TPU v7x, 32 devices: a whole 2x2x4 slice. The times are simulated.
32 devices in a mesh: batch: 2 (over x), seq: 16 (over z, y, core).
Axes of the slice: x: 2, y: 2, z: 4, core: 2. Of those that a mesh axis runs over, the one named last changes fastest.
Arguments:
- inputs: bfloat16 [2, 2048, 1024], P('batch', 'seq'), may hold values from -6 to 6
- seg_ids: int32 [2, 2048], P('batch', 'seq'), may hold values from 0 to 3, never falling along the last dimension, each value on 1 to 1024 neighbouring positions
- gain_attn: bfloat16 [1024], P('batch'), may hold values from 0.5 to 1.5
- w_query: bfloat16 [1024, 512], P('batch'), may hold values from -0.1875 to 0.1875
- w_key: bfloat16 [1024, 512], P('batch'), may hold values from -0.1875 to 0.1875
- w_value: bfloat16 [1024, 1024], P('batch'), may hold values from -0.1875 to 0.1875
- w_outgate: bfloat16 [1024, 1024], P('batch'), may hold values from -0.1875 to 0.1875
- w_rank_in: bfloat16 [1024, 16], P('batch'), may hold values from -0.1875 to 0.1875
- w_rank_out: bfloat16 [16, 512], P(None, 'batch'), may hold values from -1.5 to 1.5
- rank_bias: bfloat16 [512], P('batch'), may hold values from -0.5 to 6
- head_gain: bfloat16 [256], P('batch'), may hold values from 0.5 to 1.5
- w_output: bfloat16 [1024, 1024], P(None, 'batch'), may hold values from -0.1875 to 0.1875
- gain_ffn: bfloat16 [1024], P('batch'), may hold values from 0.5 to 1.5
- w_gate: bfloat16 [1024, 2816], P('batch'), may hold values from -0.1875 to 0.1875
- w_up: bfloat16 [1024, 2816], P('batch'), may hold values from -0.1875 to 0.1875
- w_down: bfloat16 [2816, 1024], P('batch'), may hold values from -0.109375 to 0.109375
- cotangent: bfloat16 [2, 2048, 1024], P('batch', 'seq'), may hold values from -6 to 6
Outputs:
- output: bfloat16 [2, 2048, 1024], P('batch', 'seq')
- grad_inputs: bfloat16 [2, 2048, 1024], P('batch', 'seq')
- grad_gain_attn: float32 [1024], P('batch')
- grad_w_query: float32 [1024, 512], P('batch')
- grad_w_key: float32 [1024, 512], P('batch')
- grad_w_value: float32 [1024, 1024], P('batch')
- grad_w_outgate: float32 [1024, 1024], P('batch')
- grad_w_rank_in: float32 [1024, 16], P('batch')
- grad_w_rank_out: float32 [16, 512], P(None, 'batch')
- grad_rank_bias: float32 [512], P('batch')
- grad_head_gain: float32 [256], P('batch')
- grad_w_output: float32 [1024, 1024], P(None, 'batch')
- grad_gain_ffn: float32 [1024], P('batch')
- grad_w_gate: float32 [1024, 2816], P('batch')
- grad_w_up: float32 [1024, 2816], P('batch')
- grad_w_down: float32 [2816, 1024], P('batch')
Inputs may be any that keep to these rules, and one draw needn't show every extreme that they name: `seg_ids`: along each sequence document ids never fall; each document holds 1 to 1024 tokens and one holds exactly 1024.
All inputs are finite; a program needn't handle non-finite values.
Results may differ from a plain program's by a relative error of at most 0.023.
Values may be sent and summed in bfloat16 or wider, within the bound.
A program may use at most 192 MiB of HBM per device.

v0:
```python
import jax
import jax.numpy as jnp
from jax import lax
from jax.sharding import PartitionSpec as P

HEADS = 4
DK = 128
DV = 256
SPAN = 64
KEYS = 512
VALS = 1024
norm_eps = 1e-05
head_eps = 0.1
top_prec = lax.Precision.HIGHEST
BOTH = ("batch", "seq")


def rms_scale(values_in):
    return lax.rsqrt(jnp.mean(values_in * values_in, axis=-1, keepdims=True) + norm_eps)


def head_rms(values_in):
    return lax.rsqrt(jnp.mean(values_in * values_in, axis=-1, keepdims=True) + head_eps)


def silu_grad(pre_act, sig_val):
    return sig_val * (1.0 + pre_act * (1.0 - sig_val))


def mm(eq, a, b):
    return jnp.einsum(eq, a, b, precision=top_prec)


def own_piece(shard):
    rows = shard.shape[0] // lax.axis_size("seq")
    return lax.dynamic_slice_in_dim(shard, lax.axis_index("seq") * rows, rows, 0)


def gather_rows(shards):
    pieces = [own_piece(shard) for shard in shards]
    piece = pieces[0] if len(pieces) == 1 else jnp.concatenate(pieces, axis=1)
    return lax.all_gather(piece, BOTH, axis=0, tiled=True)


def sum_rows(partial):
    piece = lax.psum_scatter(partial.astype(jnp.bfloat16), BOTH, scatter_dimension=0, tiled=True)
    return lax.all_gather(piece, "seq", axis=0, tiled=True)


def to_spans(array_in, width):
    return array_in.reshape(-1, SPAN, HEADS, width).transpose(0, 2, 1, 3)


def from_spans(array_in):
    spans, heads, span_len, width = array_in.shape
    return array_in.transpose(0, 2, 1, 3).reshape(spans * span_len, heads * width)


def per_device(
    inputs,
    seg_ids,
    gain_attn,
    w_query,
    w_key,
    w_value,
    w_outgate,
    w_rank_in,
    w_rank_out,
    rank_bias,
    head_gain,
    w_output,
    gain_ffn,
    w_gate,
    w_up,
    w_down,
    cotangent,
):
    f32 = jnp.float32
    bf16 = jnp.bfloat16
    nb = lax.axis_size("batch")
    mine_b = lax.axis_index("batch")
    place = lax.axis_index("seq")
    peers = lax.axis_size("seq")
    small = (gain_attn, gain_ffn, rank_bias, head_gain, w_rank_in, w_rank_out)
    packed = jnp.concatenate([a.reshape(-1) for a in small])
    packed = lax.all_gather(packed, "batch", axis=0)
    parts, at = ([], 0)
    for a in small:
        parts.append(packed[:, at : at + a.size])
        at += a.size
    gain_one = parts[0].reshape(-1).astype(f32)
    gain_two = parts[1].reshape(-1).astype(f32)
    bias_w = parts[2].reshape(-1).astype(f32)
    head_gain32 = parts[3].reshape(-1).astype(f32)
    rank_in_w = parts[4].reshape(-1, w_rank_in.shape[1])
    rank_out_w = (
        parts[5]
        .reshape((nb,) + w_rank_out.shape)
        .transpose(1, 0, 2)
        .reshape(w_rank_out.shape[0], -1)
        .astype(f32)
    )
    proj_w = gather_rows((w_query, w_key, w_value, w_outgate))
    output_w = gather_rows((w_output,)).reshape((nb,) + w_output.shape)
    gate_up_w = gather_rows((w_gate, w_up))
    down_w = gather_rows((w_down,))
    ff = w_gate.shape[1]
    activation = inputs[0].astype(f32)
    seg_row = seg_ids[0]
    tok_count = activation.shape[0]
    spans = tok_count // SPAN
    scale_one = rms_scale(activation)
    unit_one = activation * scale_one
    normed = (unit_one * gain_one).astype(bf16)
    low_rank = jnp.dot(normed, rank_in_w, preferred_element_type=f32)
    logits = jnp.dot(low_rank, rank_out_w, precision=top_prec) + bias_w
    decays = jax.nn.log_sigmoid(logits) / 16.0
    seg_s = seg_row.reshape(spans, SPAN)
    first_s, last_s = (seg_s[:, 0], seg_s[:, -1])
    row_pos = lax.broadcasted_iota(jnp.int32, (SPAN, SPAN), 0)
    col_pos = lax.broadcasted_iota(jnp.int32, (SPAN, SPAN), 1)
    lower = (col_pos <= row_pos).astype(f32)
    allowed = lower[None] * (seg_s[:, :, None] == seg_s[:, None, :]).astype(f32)
    allowed = allowed[:, None]
    prior = jnp.concatenate([seg_row[:1], last_s[:-1]])
    enters = (first_s == prior).astype(f32)
    within = ((seg_s == first_s[:, None]).astype(f32) * enters[:, None])[:, None, :, None]
    end_doc = (seg_s == last_s[:, None]).astype(f32)[:, None, :, None]
    cumul = mm("ts,nsc->ntc", lower, decays.reshape(spans, SPAN, KEYS))
    total_log = jnp.sum(cumul[:, -1], axis=0)
    edges = jnp.stack([seg_row[0], seg_row[-1]]).astype(f32)
    notes = lax.all_gather(jnp.concatenate([total_log, edges]), "seq", axis=0)
    all_log, firsts, lasts = (notes[:, :KEYS], notes[:, KEYS], notes[:, KEYS + 1])
    proj = jnp.dot(normed, proj_w, preferred_element_type=f32)
    queries = to_spans(proj[:, :KEYS] * DK ** (-0.5), DK)
    keys_s = to_spans(proj[:, KEYS : 2 * KEYS], DK)
    values_s = to_spans(proj[:, 2 * KEYS : 2 * KEYS + VALS], DV)
    outgate = proj[:, 2 * KEYS + VALS :]
    cumul = cumul.reshape(spans, SPAN, HEADS, DK).transpose(0, 2, 1, 3)
    last_cumul = cumul[:, :, -1:, :]
    grow = jnp.exp(cumul)
    shrink = jnp.exp(-cumul)
    to_end = jnp.exp(last_cumul - cumul) * end_doc
    query_dec = queries * grow
    key_dec = keys_s * shrink
    key_end = keys_s * to_end
    query_in = query_dec * within
    keep = jnp.exp(last_cumul[:, :, 0, :]) * within[:, :, -1]
    scores = mm("nhtc,nhsc->nhts", query_dec, key_dec) * allowed
    local_out = mm("nhts,nhsv->nhtv", scores, values_s)
    added = mm("nhsc,nhsv->nhcv", key_end, values_s)
    local_state = added[0]
    for i in range(1, spans):
        local_state = keep[i][:, :, None] * local_state + added[i]
    states = lax.all_gather(local_state.astype(bf16), "seq", axis=0)
    before = lax.broadcasted_iota(jnp.int32, (peers, peers), 1)
    row = lax.broadcasted_iota(jnp.int32, (peers, peers), 0)
    order = jnp.arange(peers)
    between = jnp.logical_and(before > row, before < place).astype(f32)
    reach = jnp.logical_and(order < place, lasts == edges[0]).astype(f32)
    weight = jnp.exp(mm("ji,ic->jc", between, all_log)) * reach[:, None]
    carried = jnp.sum(states.astype(f32) * weight.reshape(peers, HEADS, DK, 1), axis=0)
    enter_list = [carried]
    for i in range(spans - 1):
        enter_list.append(keep[i][:, :, None] * enter_list[i] + added[i])
    entered = jnp.stack(enter_list)
    attn_raw = from_spans(local_out + mm("nhtc,nhcv->nhtv", query_in, entered)).reshape(
        tok_count, HEADS, DV
    )
    head_scale = head_rms(attn_raw)
    head_norm = attn_raw * head_scale
    gate_h = outgate.reshape(tok_count, HEADS, DV)
    gate_sig = jax.nn.sigmoid(gate_h)
    gate_act = gate_h * gate_sig
    gated = (head_norm * head_gain32 * gate_act).reshape(tok_count, VALS).astype(bf16)
    out_proj = jnp.concatenate(
        [jnp.dot(gated, output_w[b], preferred_element_type=f32) for b in range(nb)], axis=1
    )
    resid = activation + out_proj
    scale_two = rms_scale(resid)
    unit_two = resid * scale_two
    normed_two = (unit_two * gain_two).astype(bf16)
    gate_up = jnp.dot(normed_two, gate_up_w, preferred_element_type=f32)
    gate_pre, up_pre = (gate_up[:, :ff], gate_up[:, ff:])
    ffn_sig = jax.nn.sigmoid(gate_pre)
    hidden = (gate_pre * ffn_sig * up_pre).astype(bf16)
    output = (resid + jnp.dot(hidden, down_w, preferred_element_type=f32)).astype(bf16)
    cot_rows = cotangent[0]
    grad_down = sum_rows(jnp.dot(hidden.T, cot_rows, preferred_element_type=f32))
    grad_hidden = jnp.dot(cot_rows, down_w.T, preferred_element_type=f32)
    grad_gate_up = jnp.concatenate(
        [
            (grad_hidden * up_pre * silu_grad(gate_pre, ffn_sig)).astype(bf16),
            (grad_hidden * gate_pre * ffn_sig).astype(bf16),
        ],
        axis=1,
    )
    grad_gu = sum_rows(jnp.dot(normed_two.T, grad_gate_up, preferred_element_type=f32))
    grad_normed_two = jnp.dot(grad_gate_up, gate_up_w.T, preferred_element_type=f32)
    grad_gain_two = jnp.sum(grad_normed_two * unit_two, axis=0)
    scaled_two = grad_normed_two * gain_two
    grad_resid = cot_rows.astype(f32) + scale_two * (
        scaled_two - unit_two * jnp.mean(scaled_two * unit_two, axis=-1, keepdims=True)
    )
    resid_bf = grad_resid.astype(bf16)
    half = resid_bf.shape[1] // nb
    halves = [resid_bf[:, b * half : (b + 1) * half] for b in range(nb)]
    grad_output = sum_rows(
        jnp.concatenate(
            [jnp.dot(gated.T, part, preferred_element_type=f32) for part in halves], axis=0
        )
    )
    grad_gated = sum(
        (jnp.dot(part, output_w[b].T, preferred_element_type=f32) for b, part in enumerate(halves))
    ).reshape(tok_count, HEADS, DV)
    grad_headgain = jnp.sum(grad_gated * head_norm * gate_act, axis=(0, 1))
    grad_gate_h = grad_gated * head_norm * head_gain32 * silu_grad(gate_h, gate_sig)
    grad_norm_h = grad_gated * head_gain32 * gate_act
    grad_attn = head_scale * (
        grad_norm_h - head_norm * jnp.mean(grad_norm_h * head_norm, axis=-1, keepdims=True)
    )
    grad_o = to_spans(grad_attn.reshape(tok_count, VALS), DV)
    reach_grad = mm("nhtc,nhtv->nhcv", query_in, grad_o)
    local_grad = reach_grad[spans - 1]
    for i in range(spans - 2, -1, -1):
        local_grad = keep[i][:, :, None] * local_grad + reach_grad[i]
    grads_in = lax.all_gather(local_grad.astype(bf16), "seq", axis=0)
    grad_scores = mm("nhtv,nhsv->nhts", grad_o, values_s) * allowed
    grad_qd = mm("nhts,nhsc->nhtc", grad_scores, key_dec)
    grad_qd = grad_qd + within * mm("nhtv,nhcv->nhtc", grad_o, entered)
    grad_kd = mm("nhts,nhtc->nhsc", grad_scores, query_dec)
    grad_v = mm("nhts,nhtv->nhsv", scores, grad_o)
    between = jnp.logical_and(before < row, before > place).astype(f32)
    reach = jnp.logical_and(order > place, firsts == edges[1]).astype(f32)
    weight = jnp.exp(mm("ji,ic->jc", between, all_log)) * reach[:, None]
    grad_end = jnp.sum(grads_in.astype(f32) * weight.reshape(peers, HEADS, DK, 1), axis=0)
    end_list = [grad_end]
    for i in range(spans - 1, 0, -1):
        end_list.append(keep[i][:, :, None] * end_list[-1] + reach_grad[i])
    ends = jnp.stack(end_list[::-1])
    grad_v = grad_v + mm("nhsc,nhcv->nhsv", key_end, ends)
    grad_ke = mm("nhsv,nhcv->nhsc", values_s, ends)
    moved = grad_ke * key_end
    grad_last = jnp.sum(moved, axis=2) + keep * jnp.sum(ends * entered, axis=3)
    grad_cumul = grad_qd * query_dec - grad_kd * key_dec - moved
    grad_d = mm("ts,nhtc->nhsc", lower, grad_cumul) + grad_last[:, :, None, :]
    grad_q = grad_qd * grow
    grad_k = grad_kd * shrink + grad_ke * to_end
    grad_logits = from_spans(grad_d) * jax.nn.sigmoid(-logits) / 16.0
    grad_bias = jnp.sum(grad_logits, axis=0)
    grad_rank_out = jnp.dot(low_rank.T, grad_logits, precision=top_prec)
    grad_low = jnp.dot(grad_logits, rank_out_w.T, precision=top_prec).astype(bf16)
    proj_grad = jnp.concatenate(
        [
            from_spans(grad_q * DK ** (-0.5)).astype(bf16),
            from_spans(grad_k).astype(bf16),
            from_spans(grad_v).astype(bf16),
            grad_gate_h.reshape(tok_count, VALS).astype(bf16),
        ],
        axis=1,
    )
    grad_proj = sum_rows(jnp.dot(normed.T, proj_grad, preferred_element_type=f32))
    grad_normed = jnp.dot(proj_grad, proj_w.T, preferred_element_type=f32) + jnp.dot(
        grad_low, rank_in_w.T, preferred_element_type=f32
    )
    grad_gain_one = jnp.sum(grad_normed * unit_one, axis=0)
    scaled_one = grad_normed * gain_one
    grad_input = (
        grad_resid
        + scale_one
        * (scaled_one - unit_one * jnp.mean(scaled_one * unit_one, axis=-1, keepdims=True))
    ).astype(bf16)
    grad_rank_in = jnp.dot(normed.T, grad_low, preferred_element_type=f32)
    by_owner = jnp.concatenate(
        [
            grad_gain_one.reshape(nb, -1),
            grad_gain_two.reshape(nb, -1),
            grad_bias.reshape(nb, -1),
            grad_headgain.reshape(nb, -1),
            grad_rank_in.reshape(nb, -1),
            grad_rank_out.reshape(w_rank_out.shape[0], nb, -1).transpose(1, 0, 2).reshape(nb, -1),
        ],
        axis=1,
    )
    owned = lax.dynamic_index_in_dim(lax.psum(by_owner, BOTH), mine_b, 0, False)
    outs, at = ([], 0)
    for a in small:
        outs.append(owned[at : at + a.size].reshape(a.shape))
        at += a.size
    g_gain_one, g_gain_two, g_bias, g_headgain, g_rank_in, g_rank_out = outs
    grad_proj = grad_proj.astype(f32)
    grad_gu = grad_gu.astype(f32)
    return (
        output[None],
        grad_input[None],
        g_gain_one,
        grad_proj[:, :KEYS],
        grad_proj[:, KEYS : 2 * KEYS],
        grad_proj[:, 2 * KEYS : 2 * KEYS + VALS],
        grad_proj[:, 2 * KEYS + VALS :],
        g_rank_in,
        g_rank_out,
        g_bias,
        g_headgain,
        grad_output.astype(f32),
        g_gain_two,
        grad_gu[:, :ff],
        grad_gu[:, ff:],
        grad_down.astype(f32),
    )


def solution(mesh):
    in_specs = (
        P("batch", "seq", None),
        P("batch", "seq"),
        P("batch"),
        P("batch", None),
        P("batch", None),
        P("batch", None),
        P("batch", None),
        P("batch", None),
        P(None, "batch"),
        P("batch"),
        P("batch"),
        P(None, "batch"),
        P("batch"),
        P("batch", None),
        P("batch", None),
        P("batch", None),
        P("batch", "seq", None),
    )
    out_specs = (
        P("batch", "seq", None),
        P("batch", "seq", None),
        P("batch"),
        P("batch", None),
        P("batch", None),
        P("batch", None),
        P("batch", None),
        P("batch", None),
        P(None, "batch"),
        P("batch"),
        P("batch"),
        P(None, "batch"),
        P("batch"),
        P("batch", None),
        P("batch", None),
        P("batch", None),
    )
    return jax.shard_map(
        per_device, mesh=mesh, in_specs=in_specs, out_specs=out_specs, check_vma=False
    )
```

profile of v0, /device:TPU:0, one launch (start us, length us, event | category | flops | bytes accessed | tf_op | source)
XLA Modules:
  0.0 1341.5 jit_solution(14421822726846353848)
XLA Ops:
  15.6 5.7 all-gather.2
  32.2 51.4 %all-gather.14.cloned.1.call-done = bf16[1024,3072]{1,0:T(8,128)(2,1)} async-done(((bf16[32,3072]{1,0:T(8,128)(2,1)}), bf16[1024,3072]{1,0:T(8,128)(2,1)}) %all-gather.14.cloned.1.call-update) | async-done | bytes 6291472 | tf_op jit(solution)/shard_map/all_gather | solution.py:42
  83.6 3.8 fusion.128
  108.8 61.4 %all-reduce = f32[8224]{0:T(1024)S(1)} all-reduce(f32[8224]{0:T(1024)S(1)} %maximum_dynamic-update-slice_fusion), channel_id=3, replica_groups=mesh['batch'=2,'seq'=16] {'seq'}, use_global_device_ids=true, to_apply=%add | all-reduce | flops 8224 | bytes 65792
  178.6 3.4 multiply_reduce_fusion.1
  190.0 19.7 %all-gather.18.cloned.1.call-done = bf16[2048,512]{1,0:T(8,128)(2,1)} async-done(((bf16[64,512]{1,0:T(8,128)(2,1)}), bf16[2048,512]{1,0:T(8,128)(2,1)}) %all-gather.18.cloned.1.call-update) | async-done | bytes 2097168 | tf_op jit(solution)/shard_map/all_gather | solution.py:42
  213.1 89.3 %all-gather.20.cloned.1.call-done = bf16[1024,5632]{1,0:T(8,128)(2,1)} async-done(((bf16[32,5632]{1,0:T(8,128)(2,1)}), bf16[1024,5632]{1,0:T(8,128)(2,1)}) %all-gather.20.cloned.1.call-update) | async-done | bytes 11534352 | tf_op jit(solution)/shard_map/all_gather | solution.py:42
  302.4 7.6 fusion.124
  310.0 61.6 %all-gather.22.cloned.1.call-done = bf16[2816,1024]{1,0:T(8,128)(2,1)} async-done(((bf16[88,1024]{1,0:T(8,128)(2,1)}), bf16[2816,1024]{1,0:T(8,128)(2,1)}) %all-gather.22.cloned.1.call-update) | async-done | bytes 5767184 | tf_op jit(solution)/shard_map/all_gather | solution.py:42
  371.7 6.8 multiply_convert_fusion.1
  378.5 4.4 multiply_reduce_fusion.4
  389.1 2.9 multiply_reduce_fusion.3
  403.1 5.3 convolution_convert_fusion.1
  414.0 35.6 %all-gather.24.cloned.1.call-done = bf16[16,4,128,256]{3,2,1,0:T(8,128)(2,1)} async-done(((bf16[1,4,128,256]{3,2,1,0:T(8,128)(2,1)}), bf16[16,4,128,256]{3,2,1,0:T(8,128)(2,1)}) %all-gather.24.cloned.1.call-update) | async-done | bytes 4194320 | tf_op jit(solution)/shard_map/all_gather | solution.py:227
  449.6 3.0 multiply_reduce_fusion
  457.5 4.5 convolution_convert_fusion.2
  463.1 7.1 convolution_convert_fusion
  471.0 118.4 %reduce-scatter.7.cloned.1.call-done = bf16[64,512]{1,0:T(8,128)(2,1)} async-done(((bf16[2048,512]{1,0:T(8,128)(2,1)}), bf16[64,512]{1,0:T(8,128)(2,1)}) %reduce-scatter.7.cloned.1.call-update) | async-done | bytes 65552 | tf_op jit(solution)/shard_map/reduce_scatter | solution.py:46
  593.4 5.1 fusion.90
  600.4 133.6 %reduce-scatter.11.cloned.1.call-done = bf16[88,1024]{1,0:T(8,128)(2,1)} async-done(((bf16[2816,1024]{1,0:T(8,128)(2,1)}), bf16[88,1024]{1,0:T(8,128)(2,1)}) %reduce-scatter.11.cloned.1.call-update) | async-done | bytes 180240 | tf_op jit(solution)/shard_map/reduce_scatter | solution.py:46
  734.1 116.5 %reduce-scatter.5.cloned.1.call-done = bf16[32,3072]{1,0:T(8,128)(2,1)} async-done(((bf16[1024,3072]{1,0:T(8,128)(2,1)}), bf16[32,3072]{1,0:T(8,128)(2,1)}) %reduce-scatter.5.cloned.1.call-update) | async-done | bytes 196624 | tf_op jit(solution)/shard_map/reduce_scatter | solution.py:46
  850.6 156.7 %reduce-scatter.9.cloned.1.call-done = bf16[32,5632]{1,0:T(8,128)(2,1)} async-done(((bf16[1024,5632]{1,0:T(8,128)(2,1)}), bf16[32,5632]{1,0:T(8,128)(2,1)}) %reduce-scatter.9.cloned.1.call-update) | async-done | bytes 360464 | tf_op jit(solution)/shard_map/reduce_scatter | solution.py:46
  1007.3 4.3 fusion.3
  1011.6 34.8 %all-gather.28.cloned.1.call-done = bf16[1024,512]{1,0:T(8,128)(2,1)} async-done(((bf16[64,512]{1,0:T(8,128)(2,1)}), bf16[1024,512]{1,0:T(8,128)(2,1)}) %all-gather.28.cloned.1.call-update) | async-done | bytes 1048592 | tf_op jit(solution)/shard_map/all_gather | solution.py:47
  1046.4 2.8 convert_element_type.216
  1050.3 123.7 %all-reduce.3.cloned.1.call-done = f32[2,13696]{1,0:T(2,128)} async-done(((f32[2,13696]{1,0:T(2,128)}), f32[2,13696]{1,0:T(2,128)}) %all-reduce.3.cloned.1.call-update) | async-done | bytes 109584 | tf_op jit(solution)/shard_map/psum | solution.py:285
  1181.2 39.9 %all-gather.32.cloned.1.call-done = bf16[1408,1024]{1,0:T(8,128)(2,1)} async-done(((bf16[88,1024]{1,0:T(8,128)(2,1)}), bf16[1408,1024]{1,0:T(8,128)(2,1)}) %all-gather.32.cloned.1.call-update) | async-done | bytes 2883600 | tf_op jit(solution)/shard_map/all_gather | solution.py:47
  1221.2 5.1 convert_element_type.220
  1226.3 41.2 %all-gather.26.cloned.1.call-done = bf16[512,3072]{1,0:T(8,128)(2,1)} async-done(((bf16[32,3072]{1,0:T(8,128)(2,1)}), bf16[512,3072]{1,0:T(8,128)(2,1)}) %all-gather.26.cloned.1.call-update) | async-done | bytes 3145744 | tf_op jit(solution)/shard_map/all_gather | solution.py:47
  1267.4 3.0 fusion.137
  1272.9 53.7 %all-gather.30.cloned.1.call-done = bf16[512,5632]{1,0:T(8,128)(2,1)} async-done(((bf16[32,5632]{1,0:T(8,128)(2,1)}), bf16[512,5632]{1,0:T(8,128)(2,1)}) %all-gather.30.cloned.1.call-update) | async-done | bytes 5767184 | tf_op jit(solution)/shard_map/all_gather | solution.py:47
  1326.6 8.1 fusion.135
  (352 shorter events, 104.9 us)
Async XLA Ops:
  7.2 97.9 %copy-start = (bf16[1408,1024]{1,0:T(8,128)(2,1)S(1)}, bf16[1408,1024]{1,0:T(8,128)(2,1)}, u32[]{:S(2)}) copy-start(bf16[1408,1024]{1,0:T(8,128)(2,1)} %param.32) | copy-start | bytes 8650756
  7.2 76.4 %copy-start.3 = (bf16[1,128,1024]{2,1,0:T(8,128)(2,1)S(1)}, bf16[1,128,1024]{2,1,0:T(8,128)(2,1)}, u32[]{:S(2)}) copy-start(bf16[1,128,1024]{2,1,0:T(8,128)(2,1)} %param.17) | copy-start | bytes 786436
  7.2 76.3 %all-gather.14.cloned.1.call-start = ((), (), s32[]{:S(2)}) async-start(), calls=%async_computation.4 | async-start | bytes 6488064 | tf_op jit(solution)/shard_map/all_gather | solution.py:42
  9.8 168.8 %all-gather.16.cloned.1.call-start = ((), (), s32[]{:S(2)}) async-start(), calls=%async_computation.5 | async-start | bytes 4456448 | tf_op jit(solution)/shard_map/all_gather | solution.py:155
  24.9 62.5 %copy-start.62 = (f32[128]{0:T(128)}, f32[128]{0:T(128)S(1)}, u32[]{:S(2)}) copy-start(f32[128]{0:T(128)S(1)} %add_rsqrt_fusion.2) | copy-start | bytes 1540
  28.4 66.7 %copy-start.56 = (f32[2,4,1,128]{3,2,1,0:T(1,128)}, f32[2,4,1,128]{3,2,1,0:T(1,128)S(1)}, u32[]{:S(2)}) copy-start(f32[2,4,1,128]{3,2,1,0:T(1,128)S(1)} %slice.232) | copy-start | bytes 12292
  31.6 63.5 %copy-start.72 = (f32[2,64]{1,0:T(2,128)}, f32[2,64]{1,0:T(2,128)S(1)}, u32[]{:S(2)}) copy-start(f32[2,64]{1,0:T(2,128)S(1)} %compare_convert_fusion) | copy-start | bytes 1540
  32.2 67.6 %copy-start.66 = (f32[4,128]{1,0:T(4,128)}, f32[4,128]{1,0:T(4,128)S(1)}, u32[]{:S(2)}) copy-start(f32[4,128]{1,0:T(4,128)S(1)} %get-tuple-element.116) | copy-start | bytes 6148
  97.6 75.9 %copy-start.75 = (s32[2]{0:T(128)S(1)}, s32[2]{0:T(128)}, u32[]{:S(2)}) copy-start(s32[2]{0:T(128)} %copy-done.74) | copy-start | bytes 28
  101.6 108.1 %all-gather.18.cloned.1.call-start = ((), (), s32[]{:S(2)}) async-start(), calls=%async_computation.6 | async-start | bytes 2162688 | tf_op jit(solution)/shard_map/all_gather | solution.py:42
  103.2 199.3 %all-gather.20.cloned.1.call-start = ((), (), s32[]{:S(2)}) async-start(), calls=%async_computation.7 | async-start | bytes 11894784 | tf_op jit(solution)/shard_map/all_gather | solution.py:42
  105.0 266.6 %all-gather.22.cloned.1.call-start = ((), (), s32[]{:S(2)}) async-start(), calls=%async_computation.8 | async-start | bytes 5947392 | tf_op jit(solution)/shard_map/all_gather | solution.py:42
  105.8 343.8 %all-gather.24.cloned.1.call-start = ((), (), s32[]{:S(2)}) async-start(), calls=%async_computation.9 | async-start | bytes 4456448 | tf_op jit(solution)/shard_map/all_gather | solution.py:227
  173.6 223.7 %copy-start.69 = (f32[2,64]{1,0:T(2,128)}, f32[2,64]{1,0:T(2,128)S(1)}, u32[]{:S(2)}) copy-start(f32[2,64]{1,0:T(2,128)S(1)} %compare_select_fusion.3) | copy-start | bytes 1540
  213.1 169.8 %copy-start.64 = (f32[128]{0:T(128)}, f32[128]{0:T(128)S(1)}, u32[]{:S(2)}) copy-start(f32[128]{0:T(128)S(1)} %add_rsqrt_fusion.1) | copy-start | bytes 1540
  400.4 189.0 %reduce-scatter.7.cloned.1.call-start = ((), (), s32[]{:S(2)}) async-start(), calls=%async_computation.13 | async-start | bytes 2162688 | tf_op jit(solution)/shard_map/reduce_scatter | solution.py:46
  402.9 331.2 %reduce-scatter.11.cloned.1.call-start = ((), (), s32[]{:S(2)}) async-start(), calls=%async_computation.17 | async-start | bytes 5947392 | tf_op jit(solution)/shard_map/reduce_scatter | solution.py:46
  408.5 442.1 %reduce-scatter.5.cloned.1.call-start = ((), (), s32[]{:S(2)}) async-start(), calls=%async_computation.11 | async-start | bytes 6488064 | tf_op jit(solution)/shard_map/reduce_scatter | solution.py:46
  412.6 40.1 %copy-start.67 = (f32[4,128]{1,0:T(4,128)S(1)}, f32[4,128]{1,0:T(4,128)}, u32[]{:S(2)}) copy-start(f32[4,128]{1,0:T(4,128)} %copy-done.66) | copy-start | bytes 6148
  462.1 545.2 %reduce-scatter.9.cloned.1.call-start = ((), (), s32[]{:S(2)}) async-start(), calls=%async_computation.15 | async-start | bytes 11894784 | tf_op jit(solution)/shard_map/reduce_scatter | solution.py:46
  470.3 119.4 %copy-start.13 = (f32[1,4,128,256]{3,2,1,0:T(8,128)S(1)}, f32[1,4,128,256]{3,2,1,0:T(8,128)}, u32[]{:S(2)}) copy-start(f32[1,4,128,256]{3,2,1,0:T(8,128)} %copy-done.11) | copy-start | bytes 1572868
  470.3 119.4 %copy-start.15 = (f32[1,4,128,256]{3,2,1,0:T(8,128)S(1)}, f32[1,4,128,256]{3,2,1,0:T(8,128)}, u32[]{:S(2)}) copy-start(f32[1,4,128,256]{3,2,1,0:T(8,128)} %copy-done.14) | copy-start | bytes 1572868
  470.3 119.7 %copy-start.77 = (f32[2]{0:T(128)S(1)}, f32[2]{0:T(128)}, u32[]{:S(2)}) copy-start(f32[2]{0:T(128)} %copy-done.76) | copy-start | bytes 28
  470.3 122.4 %copy-start.59 = (bf16[2,8,2,256]{3,1,2,0:T(8,128)(2,1)S(1)}, bf16[2,8,2,256]{3,1,2,0:T(8,128)(2,1)}, u32[]{:S(2)}) copy-start(bf16[2,8,2,256]{3,1,2,0:T(8,128)(2,1)} %copy-done.58) | copy-start | bytes 49156
  470.3 576.1 %all-gather.28.cloned.1.call-start = ((), (), s32[]{:S(2)}) async-start(), calls=%async_computation.14 | async-start | bytes 1114112 | tf_op jit(solution)/shard_map/all_gather | solution.py:47
  589.4 584.6 %all-reduce.3.cloned.1.call-start = ((), (), s32[]{:S(2)}) async-start(), calls=%async_computation.10 | async-start | bytes 219136 | tf_op jit(solution)/shard_map/psum | solution.py:285
  598.6 408.8 %copy-start.23 = (bf16[128,2816]{1,0:T(8,128)(2,1)S(1)}, bf16[128,2816]{1,0:T(8,128)(2,1)}, u32[]{:S(2)}) copy-start(bf16[128,2816]{1,0:T(8,128)(2,1)} %get-tuple-element.102) | copy-start | bytes 2162692
  600.3 620.9 %all-gather.32.cloned.1.call-start = ((), (), s32[]{:S(2)}) async-start(), calls=%async_computation.18 | async-start | bytes 3063808 | tf_op jit(solution)/shard_map/all_gather | solution.py:47
  734.1 533.4 %all-gather.26.cloned.1.call-start = ((), (), s32[]{:S(2)}) async-start(), calls=%async_computation.12 | async-start | bytes 3342336 | tf_op jit(solution)/shard_map/all_gather | solution.py:47
  850.6 476.0 %all-gather.30.cloned.1.call-start = ((), (), s32[]{:S(2)}) async-start(), calls=%async_computation.16 | async-start | bytes 6127616 | tf_op jit(solution)/shard_map/all_gather | solution.py:47
  1011.6 37.6 %copy-start.36 = (bf16[1,128,1024]{2,1,0:T(8,128)(2,1)S(1)}, bf16[1,128,1024]{2,1,0:T(8,128)(2,1)}, u32[]{:S(2)}) copy-start(bf16[1,128,1024]{2,1,0:T(8,128)(2,1)} %param.33) | copy-start | bytes 786436
  1011.6 37.6 %copy-start.80 = (f32[128]{0:T(128)S(1)}, f32[128]{0:T(128)}, u32[]{:S(2)}) copy-start(f32[128]{0:T(128)} %copy-done.79) | copy-start | bytes 1540
  (65 other events, 253.0 us)
Sparse Core Ops, SparseCore 0:
  11.5 72.0 all-gather.13
  101.7 49.5 all-gather.15
  154.8 54.8 all-gather.17
  213.0 89.3 all-gather.19
  305.7 65.8 all-gather.21
  400.5 49.0 all-gather.23
  452.4 136.8 reduce-scatter.6
  592.2 141.7 reduce-scatter.10
  739.7 110.8 reduce-scatter.4
  852.7 154.5 reduce-scatter.8
  1009.5 36.8 all-gather.27
  1052.4 121.5 all-reduce.2
  1176.3 44.8 all-gather.31
  1223.3 44.0 all-gather.25
  1269.6 56.9 all-gather.29
where the time goes:
time: 1350 us; the launch traced here: 1340 us
  waiting for transfers between devices  1080 us (80%)
  matrix products  79.5 us (6%)
  blocking collectives  67.1 us (5%)
  local copies, waits for them, and re-layouts  60.4 us (4%)
  other arithmetic  41 us (3%)
  between operations  16.1 us (1%)
    reduce_scatter x4, waiting for transfers between devices, sum_rows(): lax.psum_scatter(partial.astype(jnp.bfloat16), BOTH, scatter_dimension=0,...  525 us
    all_gather x4, waiting for transfers between devices, gather_rows(): return lax.all_gather(piece, BOTH, axis=0, tiled=True)  222 us
    all_gather x4, waiting for transfers between devices, sum_rows(): return lax.all_gather(piece, 'seq', axis=0, tiled=True)  170 us
    psum x1, waiting for transfers between devices, per_device(): owned = lax.dynamic_index_in_dim(lax.psum(by_owner, BOTH), mine_b, 0, False)  124 us
    unnamed x1, blocking collectives  61.4 us
    all_gather x1, waiting for transfers between devices, per_device(): grads_in = lax.all_gather(local_grad.astype(bf16), 'seq', axis=0)  35.6 us
  transfers between devices with their start and end apart: 15, of which 14 were waited for; matrix products, arithmetic and copies ran while one was open for 9% of the time, Pallas kernels for 0%

commit v1 on v0

--- a/solution.py
+++ b/solution.py
@@ -13,6 +13,12 @@
 head_eps = 0.1
 top_prec = lax.Precision.HIGHEST
 BOTH = ("batch", "seq")
+
+
+def add_all(x, axis):
+    blocks = lax.all_gather(x, axis, axis=0, tiled=False)
+    acc = blocks.sum(axis=0)
+    return acc
 
 
 def rms_scale(values_in):
@@ -282,7 +288,7 @@
         ],
         axis=1,
     )
-    owned = lax.dynamic_index_in_dim(lax.psum(by_owner, BOTH), mine_b, 0, False)
+    owned = lax.dynamic_index_in_dim(add_all(by_owner, BOTH), mine_b, 0, False)
     outs, at = ([], 0)
     for a in small:
         outs.append(owned[at : at + a.size].reshape(a.shape))

time: 1350 us -> 1280 us (0.948)
  waiting for transfers between devices: 1080 us -> 1010 us
    psum x1 -> x0, waiting for transfers between devices: 124 us -> none  [per_device(): owned = lax.dynamic_index_in_dim(lax.psum(by_owner, BOTH), mine_b, 0, False)]
    all_gather x0 -> x1, waiting for transfers between devices: none -> 58.6 us  [add_all(): blocks = lax.all_gather(x, axis, axis=0, tiled=False)]
where the time goes in v1:
time: 1280 us; the launch traced here: 1270 us
  waiting for transfers between devices  1010 us (79%)
  matrix products  79.5 us (6%)
  blocking collectives  67.1 us (5%)
  local copies, waits for them, and re-layouts  56.8 us (4%)
  other arithmetic  44.1 us (3%)
  between operations  16.1 us (1%)
    reduce_scatter x4, waiting for transfers between devices, sum_rows(): lax.psum_scatter(partial.astype(jnp.bfloat16), BOTH, scatter_dimension=0,...  525 us
    all_gather x4, waiting for transfers between devices, gather_rows(): return lax.all_gather(piece, BOTH, axis=0, tiled=True)  222 us
    all_gather x4, waiting for transfers between devices, sum_rows(): return lax.all_gather(piece, 'seq', axis=0, tiled=True)  168 us
    unnamed x1, blocking collectives  61.4 us
    all_gather x1, waiting for transfers between devices, add_all(): blocks = lax.all_gather(x, axis, axis=0, tiled=False)  58.6 us
    all_gather x1, waiting for transfers between devices, per_device(): grads_in = lax.all_gather(local_grad.astype(bf16), 'seq', axis=0)  35.6 us
  transfers between devices with their start and end apart: 15, of which 14 were waited for; matrix products, arithmetic and copies ran while one was open for 9% of the time, Pallas kernels for 0%

profile of v1, /device:TPU:0, one launch (start us, length us, event | category | flops | bytes accessed | tf_op | source)
XLA Modules:
  0.0 1273.8 jit_solution(15487395174602288925)
XLA Ops:
  15.6 5.7 all-gather.3
  32.2 51.4 %all-gather.17.cloned.1.call-done = bf16[1024,3072]{1,0:T(8,128)(2,1)} async-done(((bf16[32,3072]{1,0:T(8,128)(2,1)}), bf16[1024,3072]{1,0:T(8,128)(2,1)}) %all-gather.17.cloned.1.call-update) | async-done | bytes 6291472 | tf_op jit(solution)/shard_map/all_gather | solution.py:48
  83.6 3.8 fusion.128
  108.8 61.4 %all-reduce = f32[8224]{0:T(1024)S(1)} all-reduce(f32[8224]{0:T(1024)S(1)} %maximum_dynamic-update-slice_fusion), channel_id=3, replica_groups=mesh['batch'=2,'seq'=16] {'seq'}, use_global_device_ids=true, to_apply=%add | all-reduce | flops 8224 | bytes 65792
  178.7 3.4 multiply_reduce_fusion.1
  190.1 19.5 %all-gather.21.cloned.1.call-done = bf16[2048,512]{1,0:T(8,128)(2,1)} async-done(((bf16[64,512]{1,0:T(8,128)(2,1)}), bf16[2048,512]{1,0:T(8,128)(2,1)}) %all-gather.21.cloned.1.call-update) | async-done | bytes 2097168 | tf_op jit(solution)/shard_map/all_gather | solution.py:48
  213.1 89.3 %all-gather.23.cloned.1.call-done = bf16[1024,5632]{1,0:T(8,128)(2,1)} async-done(((bf16[32,5632]{1,0:T(8,128)(2,1)}), bf16[1024,5632]{1,0:T(8,128)(2,1)}) %all-gather.23.cloned.1.call-update) | async-done | bytes 11534352 | tf_op jit(solution)/shard_map/all_gather | solution.py:48
  302.4 7.6 fusion.124
  310.0 61.6 %all-gather.25.cloned.1.call-done = bf16[2816,1024]{1,0:T(8,128)(2,1)} async-done(((bf16[88,1024]{1,0:T(8,128)(2,1)}), bf16[2816,1024]{1,0:T(8,128)(2,1)}) %all-gather.25.cloned.1.call-update) | async-done | bytes 5767184 | tf_op jit(solution)/shard_map/all_gather | solution.py:48
  371.6 6.8 multiply_convert_fusion.1
  378.5 4.4 multiply_reduce_fusion.4
  389.1 2.9 multiply_reduce_fusion.3
  403.1 5.3 convolution_convert_fusion.1
  414.0 35.6 %all-gather.27.cloned.1.call-done = bf16[16,4,128,256]{3,2,1,0:T(8,128)(2,1)} async-done(((bf16[1,4,128,256]{3,2,1,0:T(8,128)(2,1)}), bf16[16,4,128,256]{3,2,1,0:T(8,128)(2,1)}) %all-gather.27.cloned.1.call-update) | async-done | bytes 4194320 | tf_op jit(solution)/shard_map/all_gather | solution.py:233
  449.7 3.0 multiply_reduce_fusion
  457.6 4.5 convolution_convert_fusion.2
  463.2 7.1 convolution_convert_fusion
  471.0 118.4 %reduce-scatter.7.cloned.1.call-done = bf16[64,512]{1,0:T(8,128)(2,1)} async-done(((bf16[2048,512]{1,0:T(8,128)(2,1)}), bf16[64,512]{1,0:T(8,128)(2,1)}) %reduce-scatter.7.cloned.1.call-update) | async-done | bytes 65552 | tf_op jit(solution)/shard_map/reduce_scatter | solution.py:52
  593.4 5.1 fusion.90
  600.4 133.4 %reduce-scatter.11.cloned.1.call-done = bf16[88,1024]{1,0:T(8,128)(2,1)} async-done(((bf16[2816,1024]{1,0:T(8,128)(2,1)}), bf16[88,1024]{1,0:T(8,128)(2,1)}) %reduce-scatter.11.cloned.1.call-update) | async-done | bytes 180240 | tf_op jit(solution)/shard_map/reduce_scatter | solution.py:52
  733.9 116.5 %reduce-scatter.5.cloned.1.call-done = bf16[32,3072]{1,0:T(8,128)(2,1)} async-done(((bf16[1024,3072]{1,0:T(8,128)(2,1)}), bf16[32,3072]{1,0:T(8,128)(2,1)}) %reduce-scatter.5.cloned.1.call-update) | async-done | bytes 196624 | tf_op jit(solution)/shard_map/reduce_scatter | solution.py:52
  850.5 156.3 %reduce-scatter.9.cloned.1.call-done = bf16[32,5632]{1,0:T(8,128)(2,1)} async-done(((bf16[1024,5632]{1,0:T(8,128)(2,1)}), bf16[32,5632]{1,0:T(8,128)(2,1)}) %reduce-scatter.9.cloned.1.call-update) | async-done | bytes 360464 | tf_op jit(solution)/shard_map/reduce_scatter | solution.py:52
  1006.9 4.3 fusion.3
  1011.1 34.8 %all-gather.31.cloned.1.call-done = bf16[1024,512]{1,0:T(8,128)(2,1)} async-done(((bf16[64,512]{1,0:T(8,128)(2,1)}), bf16[1024,512]{1,0:T(8,128)(2,1)}) %all-gather.31.cloned.1.call-update) | async-done | bytes 1048592 | tf_op jit(solution)/shard_map/all_gather | solution.py:53
  1049.8 58.6 %all-gather.37.cloned.1.call-done = f32[32,2,13696]{2,1,0:T(2,128)} async-done(((f32[1,2,13696]{2,1,0:T(2,128)}), f32[32,2,13696]{2,1,0:T(2,128)}) %all-gather.37.cloned.1.call-update) | async-done | bytes 3506192 | tf_op jit(solution)/shard_map/all_gather | solution.py:19
  1108.4 3.0 reduce_sum.177
  1115.0 38.5 %all-gather.35.cloned.1.call-done = bf16[1408,1024]{1,0:T(8,128)(2,1)} async-done(((bf16[88,1024]{1,0:T(8,128)(2,1)}), bf16[1408,1024]{1,0:T(8,128)(2,1)}) %all-gather.35.cloned.1.call-update) | async-done | bytes 2883600 | tf_op jit(solution)/shard_map/all_gather | solution.py:53
  1153.5 5.1 convert_element_type.220
  1158.6 41.2 %all-gather.29.cloned.1.call-done = bf16[512,3072]{1,0:T(8,128)(2,1)} async-done(((bf16[32,3072]{1,0:T(8,128)(2,1)}), bf16[512,3072]{1,0:T(8,128)(2,1)}) %all-gather.29.cloned.1.call-update) | async-done | bytes 3145744 | tf_op jit(solution)/shard_map/all_gather | solution.py:53
  1199.8 3.0 fusion.137
  1205.2 53.7 %all-gather.33.cloned.1.call-done = bf16[512,5632]{1,0:T(8,128)(2,1)} async-done(((bf16[32,5632]{1,0:T(8,128)(2,1)}), bf16[512,5632]{1,0:T(8,128)(2,1)}) %all-gather.33.cloned.1.call-update) | async-done | bytes 5767184 | tf_op jit(solution)/shard_map/all_gather | solution.py:53
  1258.9 8.1 fusion.135
  (353 shorter events, 104.2 us)
Async XLA Ops:
  7.2 97.9 %copy-start = (bf16[1408,1024]{1,0:T(8,128)(2,1)S(1)}, bf16[1408,1024]{1,0:T(8,128)(2,1)}, u32[]{:S(2)}) copy-start(bf16[1408,1024]{1,0:T(8,128)(2,1)} %param.32) | copy-start | bytes 8650756
  7.2 76.3 %copy-start.3 = (bf16[1,128,1024]{2,1,0:T(8,128)(2,1)S(1)}, bf16[1,128,1024]{2,1,0:T(8,128)(2,1)}, u32[]{:S(2)}) copy-start(bf16[1,128,1024]{2,1,0:T(8,128)(2,1)} %param.17) | copy-start | bytes 786436
  7.2 76.3 %all-gather.17.cloned.1.call-start = ((), (), s32[]{:S(2)}) async-start(), calls=%async_computation.4 | async-start | bytes 6488064 | tf_op jit(solution)/shard_map/all_gather | solution.py:48
  9.8 168.9 %all-gather.19.cloned.1.call-start = ((), (), s32[]{:S(2)}) async-start(), calls=%async_computation.5 | async-start | bytes 4456448 | tf_op jit(solution)/shard_map/all_gather | solution.py:161
  24.9 62.5 %copy-start.62 = (f32[128]{0:T(128)}, f32[128]{0:T(128)S(1)}, u32[]{:S(2)}) copy-start(f32[128]{0:T(128)S(1)} %add_rsqrt_fusion.2) | copy-start | bytes 1540
  28.4 66.7 %copy-start.56 = (f32[2,4,1,128]{3,2,1,0:T(1,128)}, f32[2,4,1,128]{3,2,1,0:T(1,128)S(1)}, u32[]{:S(2)}) copy-start(f32[2,4,1,128]{3,2,1,0:T(1,128)S(1)} %slice.232) | copy-start | bytes 12292
  31.6 63.5 %copy-start.72 = (f32[2,64]{1,0:T(2,128)}, f32[2,64]{1,0:T(2,128)S(1)}, u32[]{:S(2)}) copy-start(f32[2,64]{1,0:T(2,128)S(1)} %compare_convert_fusion) | copy-start | bytes 1540
  32.2 67.6 %copy-start.66 = (f32[4,128]{1,0:T(4,128)}, f32[4,128]{1,0:T(4,128)S(1)}, u32[]{:S(2)}) copy-start(f32[4,128]{1,0:T(4,128)S(1)} %get-tuple-element.116) | copy-start | bytes 6148
  97.6 76.1 %copy-start.75 = (s32[2]{0:T(128)S(1)}, s32[2]{0:T(128)}, u32[]{:S(2)}) copy-start(s32[2]{0:T(128)} %copy-done.74) | copy-start | bytes 28
  101.6 108.1 %all-gather.21.cloned.1.call-start = ((), (), s32[]{:S(2)}) async-start(), calls=%async_computation.6 | async-start | bytes 2162688 | tf_op jit(solution)/shard_map/all_gather | solution.py:48
  103.2 199.2 %all-gather.23.cloned.1.call-start = ((), (), s32[]{:S(2)}) async-start(), calls=%async_computation.7 | async-start | bytes 11894784 | tf_op jit(solution)/shard_map/all_gather | solution.py:48
  105.0 266.6 %all-gather.25.cloned.1.call-start = ((), (), s32[]{:S(2)}) async-start(), calls=%async_computation.8 | async-start | bytes 5947392 | tf_op jit(solution)/shard_map/all_gather | solution.py:48
  105.8 343.8 %all-gather.27.cloned.1.call-start = ((), (), s32[]{:S(2)}) async-start(), calls=%async_computation.9 | async-start | bytes 4456448 | tf_op jit(solution)/shard_map/all_gather | solution.py:233
  173.8 223.6 %copy-start.69 = (f32[2,64]{1,0:T(2,128)}, f32[2,64]{1,0:T(2,128)S(1)}, u32[]{:S(2)}) copy-start(f32[2,64]{1,0:T(2,128)S(1)} %compare_select_fusion.3) | copy-start | bytes 1540
  213.1 169.8 %copy-start.64 = (f32[128]{0:T(128)}, f32[128]{0:T(128)S(1)}, u32[]{:S(2)}) copy-start(f32[128]{0:T(128)S(1)} %add_rsqrt_fusion.1) | copy-start | bytes 1540
  400.4 189.0 %reduce-scatter.7.cloned.1.call-start = ((), (), s32[]{:S(2)}) async-start(), calls=%async_computation.12 | async-start | bytes 2162688 | tf_op jit(solution)/shard_map/reduce_scatter | solution.py:52
  402.9 330.9 %reduce-scatter.11.cloned.1.call-start = ((), (), s32[]{:S(2)}) async-start(), calls=%async_computation.16 | async-start | bytes 5947392 | tf_op jit(solution)/shard_map/reduce_scatter | solution.py:52
  408.5 441.9 %reduce-scatter.5.cloned.1.call-start = ((), (), s32[]{:S(2)}) async-start(), calls=%async_computation.10 | async-start | bytes 6488064 | tf_op jit(solution)/shard_map/reduce_scatter | solution.py:52
  412.6 40.1 %copy-start.67 = (f32[4,128]{1,0:T(4,128)S(1)}, f32[4,128]{1,0:T(4,128)}, u32[]{:S(2)}) copy-start(f32[4,128]{1,0:T(4,128)} %copy-done.66) | copy-start | bytes 6148
  462.1 544.7 %reduce-scatter.9.cloned.1.call-start = ((), (), s32[]{:S(2)}) async-start(), calls=%async_computation.14 | async-start | bytes 11894784 | tf_op jit(solution)/shard_map/reduce_scatter | solution.py:52
  470.3 119.4 %copy-start.13 = (f32[1,4,128,256]{3,2,1,0:T(8,128)S(1)}, f32[1,4,128,256]{3,2,1,0:T(8,128)}, u32[]{:S(2)}) copy-start(f32[1,4,128,256]{3,2,1,0:T(8,128)} %copy-done.11) | copy-start | bytes 1572868
  470.3 119.4 %copy-start.15 = (f32[1,4,128,256]{3,2,1,0:T(8,128)S(1)}, f32[1,4,128,256]{3,2,1,0:T(8,128)}, u32[]{:S(2)}) copy-start(f32[1,4,128,256]{3,2,1,0:T(8,128)} %copy-done.14) | copy-start | bytes 1572868
  470.3 119.7 %copy-start.77 = (f32[2]{0:T(128)S(1)}, f32[2]{0:T(128)}, u32[]{:S(2)}) copy-start(f32[2]{0:T(128)} %copy-done.76) | copy-start | bytes 28
  470.4 122.4 %copy-start.59 = (bf16[2,8,2,256]{3,1,2,0:T(8,128)(2,1)S(1)}, bf16[2,8,2,256]{3,1,2,0:T(8,128)(2,1)}, u32[]{:S(2)}) copy-start(bf16[2,8,2,256]{3,1,2,0:T(8,128)(2,1)} %copy-done.58) | copy-start | bytes 49156
  470.4 575.6 %all-gather.31.cloned.1.call-start = ((), (), s32[]{:S(2)}) async-start(), calls=%async_computation.13 | async-start | bytes 1114112 | tf_op jit(solution)/shard_map/all_gather | solution.py:53
  589.4 519.0 %all-gather.37.cloned.1.call-start = ((), (), s32[]{:S(2)}) async-start(), calls=%async_computation.18 | async-start | bytes 3615744 | tf_op jit(solution)/shard_map/all_gather | solution.py:19
  598.6 408.2 %copy-start.23 = (bf16[128,2816]{1,0:T(8,128)(2,1)S(1)}, bf16[128,2816]{1,0:T(8,128)(2,1)}, u32[]{:S(2)}) copy-start(bf16[128,2816]{1,0:T(8,128)(2,1)} %get-tuple-element.102) | copy-start | bytes 2162692
  600.4 553.1 %all-gather.35.cloned.1.call-start = ((), (), s32[]{:S(2)}) async-start(), calls=%async_computation.17 | async-start | bytes 3063808 | tf_op jit(solution)/shard_map/all_gather | solution.py:53
  733.9 465.9 %all-gather.29.cloned.1.call-start = ((), (), s32[]{:S(2)}) async-start(), calls=%async_computation.11 | async-start | bytes 3342336 | tf_op jit(solution)/shard_map/all_gather | solution.py:53
  850.5 408.5 %all-gather.33.cloned.1.call-start = ((), (), s32[]{:S(2)}) async-start(), calls=%async_computation.15 | async-start | bytes 6127616 | tf_op jit(solution)/shard_map/all_gather | solution.py:53
  1011.1 37.7 %copy-start.36 = (bf16[1,128,1024]{2,1,0:T(8,128)(2,1)S(1)}, bf16[1,128,1024]{2,1,0:T(8,128)(2,1)}, u32[]{:S(2)}) copy-start(bf16[1,128,1024]{2,1,0:T(8,128)(2,1)} %param.33) | copy-start | bytes 786436
  1011.1 37.7 %copy-start.80 = (f32[128]{0:T(128)S(1)}, f32[128]{0:T(128)}, u32[]{:S(2)}) copy-start(f32[128]{0:T(128)} %copy-done.79) | copy-start | bytes 1540
  (65 other events, 253.1 us)
Sparse Core Ops, SparseCore 0:
  11.5 72.0 all-gather.16
  101.7 49.5 all-gather.18
  154.8 54.8 all-gather.20
  213.0 89.3 all-gather.22
  305.7 65.8 all-gather.24
  400.5 49.0 all-gather.26
  452.5 136.8 reduce-scatter.6
  592.3 141.4 reduce-scatter.10
  739.5 110.9 reduce-scatter.4
  852.6 154.1 reduce-scatter.8
  1009.0 36.9 all-gather.30
  1049.4 58.9 all-gather.36
  1110.7 42.7 all-gather.34
  1155.6 44.0 all-gather.28
  1201.9 56.9 all-gather.32
